TPU v7x, 256 devices: a whole 4x4x8 slice. The times are simulated.
256 devices in a mesh: lat: 8 (over x, z_hi), lon: 32 (over z_lo, y, core).
Axes of the slice: x: 4, y: 4, z: 8 (z_hi: 2, z_lo: 4; z = z_hi * 4 + z_lo), core: 2. Of those that a mesh axis runs over, the one named last changes fastest.
Arguments:
- fields: bfloat16 [64, 1024, 768], P('lat', 'lon'), may hold values from -60 to 60
- conv_kernel: float32 [3, 3, 768], replicated, may hold values from -1 to 1
- layer_norm_gain: float32 [768], replicated, may hold values from 0.1 to 1.9
- qkv_weight: bfloat16 [768, 2304], replicated, may hold values from -0.21875 to 0.21875
- out_weight: bfloat16 [768, 768], replicated, may hold values from -0.21875 to 0.21875
- score_bias: float32 [24, 64, 64], replicated, may hold values from -4 to 400
- pattern: int32 [8, 32, 256], P('lat', 'lon'), may hold values from 0 to 255, each once within a row
- cotangent: bfloat16 [64, 1024, 768], P('lat', 'lon'), may hold values from -6 to 6
Outputs:
- block_out: bfloat16 [64, 1024, 768], P('lat', 'lon')
- grad_fields: bfloat16 [64, 1024, 768], P('lat', 'lon')
- grad_project: float32 [768, 768], P('lat', 'lon')
- grad_kernel: float32 [3, 3, 768], replicated
- gain_gradient: float32 [768], replicated
Inputs may be any that keep to these rules, and one draw needn't show every extreme that they name: pattern[a, b, :] lists each of the 256 cells of block (a, b) once.
All inputs are finite; a program needn't handle non-finite values.
Results may differ from a plain program's by a relative error of at most 0.028.
Values may be sent and summed in bfloat16 or wider, within the bound.
A program may use at most 128 MiB of HBM per device.

v0:
```python
import math
import jax
import jax.numpy as jnp
from jax import lax
from jax.sharding import PartitionSpec as P

HEADS = 24
HEAD_DIM = 32
GROUP = 64
epsilon = 1e-05


def extended(array, sides, width, wrap):
    for axis, dim in sides:
        peers, length = (lax.axis_size(axis), array.shape[dim])
        up = [(i, (i + 1) % peers) for i in range(peers if wrap else peers - 1)]
        down = [(j, i) for i, j in up]
        last = lax.slice_in_dim(array, length - width, length, axis=dim)
        first = lax.slice_in_dim(array, 0, width, axis=dim)
        before = lax.ppermute(last, axis, up)
        after = lax.ppermute(first, axis, down)
        array = jnp.concatenate([before, array, after], axis=dim)
    return array


def widened(field):
    beside_all = extended(field, (("lon", 1),), 1, True)
    return extended(beside_all, (("lat", 0),), 1, False)


def apply_taps(padded, conv_kernel, lat_rows, lon_cols):
    summed = jnp.zeros((lat_rows, lon_cols, padded.shape[2]), jnp.float32)
    for lat_tap in range(3):
        for lon_tap in range(3):
            summed = (
                summed
                + conv_kernel[lat_tap, lon_tap]
                * padded[lat_tap : lat_tap + lat_rows, lon_tap : lon_tap + lon_cols]
            )
    return summed


def to_owner(packed):
    arrived = lax.all_to_all(
        lax.all_to_all(packed, "lat", split_axis=0, concat_axis=3, tiled=True),
        "lon",
        split_axis=1,
        concat_axis=4,
        tiled=True,
    )
    return arrived.reshape(-1, arrived.shape[-1])


def to_grid(packed):
    arrived = lax.all_to_all(
        lax.all_to_all(packed, "lat", split_axis=3, concat_axis=0, tiled=True),
        "lon",
        split_axis=4,
        concat_axis=1,
        tiled=True,
    )
    return arrived.reshape(-1, arrived.shape[-1])


def attention_probs(queries, key_rows, score_bias):
    scores = jnp.einsum("gihd,gjhd->ghij", queries, key_rows, preferred_element_type=jnp.float32)
    scores = scores * queries.shape[-1] ** (-0.5) + score_bias[None]
    peak = jnp.max(scores, axis=-1, keepdims=True)
    lifted = jnp.exp(scores - peak)
    return lifted / jnp.sum(lifted, axis=-1, keepdims=True)


def body(
    fields, conv_kernel, layer_norm_gain, qkv_weight, out_weight, score_bias, pattern, cotangent
):
    lat_rows, lon_cols, feature_count = fields.shape
    cell_count = lat_rows * lon_cols
    lat_count = lax.axis_size("lat")
    lon_count = lax.axis_size("lon")
    slot_count = cell_count // (lat_count * lon_count)
    scale_everywhere = 1.0 / math.sqrt(cell_count * lat_count * lon_count)
    head_scale = HEAD_DIM ** (-0.5)
    group_count = cell_count // GROUP
    slot_order = pattern.reshape(cell_count)
    inverse = (
        jnp.zeros((cell_count,), jnp.int32)
        .at[slot_order]
        .set(jnp.arange(cell_count, dtype=jnp.int32))
    )

    def outward(field):
        picked = jnp.take(field.reshape(cell_count, feature_count), slot_order, axis=0)
        return picked.reshape(lat_count, lon_count, slot_count, 1, 1, feature_count)

    def inward(grouped):
        return grouped.reshape(1, 1, slot_count, lat_count, lon_count, grouped.shape[-1])

    def homeward(flat):
        return jnp.take(flat, inverse, axis=0).reshape(lat_rows, lon_cols, feature_count)

    padded_fields = widened(fields)
    state_h = (
        fields.astype(jnp.float32) + apply_taps(padded_fields, conv_kernel, lat_rows, lon_cols)
    ).astype(jnp.bfloat16)
    state_f = state_h.astype(jnp.float32)
    mean_h = jnp.mean(state_f, axis=-1, keepdims=True)
    mean_removed = state_f - mean_h
    var_h = jnp.mean(mean_removed * mean_removed, axis=-1, keepdims=True)
    inverse_deviation = lax.rsqrt(var_h + epsilon)
    standardized_input = mean_removed * inverse_deviation
    normalized_fields = (standardized_input * layer_norm_gain).astype(jnp.bfloat16)
    normed_g = to_owner(outward(normalized_fields))
    cot_g = to_owner(outward(cotangent))
    qkv_rows = jnp.dot(normed_g, qkv_weight, preferred_element_type=jnp.float32).astype(
        jnp.bfloat16
    )
    split_rows = qkv_rows.reshape(group_count, GROUP, 3, HEADS, HEAD_DIM)
    queries = split_rows[:, :, 0]
    key_rows = split_rows[:, :, 1]
    value_rows = split_rows[:, :, 2]
    probs = attention_probs(queries, key_rows, score_bias)
    probs_low = probs.astype(jnp.bfloat16)
    attended = jnp.einsum(
        "ghij,gjhd->gihd", probs_low, value_rows, preferred_element_type=jnp.float32
    )
    attended = attended.astype(jnp.bfloat16).reshape(cell_count, feature_count)
    mixed = jnp.dot(attended, out_weight, preferred_element_type=jnp.float32).astype(jnp.bfloat16)
    mixed_flat = to_grid(inward(mixed))
    rows_summed = lax.psum_scatter(
        lax.dot_general(
            attended, cot_g, (((0,), (0,)), ((), ())), preferred_element_type=jnp.float32
        ).astype(jnp.bfloat16),
        "lat",
        scatter_dimension=0,
        tiled=True,
    )
    grad_project = (
        lax.psum_scatter(rows_summed, "lon", scatter_dimension=1, tiled=True).astype(jnp.float32)
        * scale_everywhere
    )
    grad_att = lax.dot_general(
        cot_g, out_weight, (((1,), (1,)), ((), ())), preferred_element_type=jnp.float32
    ).astype(jnp.bfloat16)
    grad_heads = grad_att.reshape(group_count, GROUP, HEADS, HEAD_DIM)
    held_query, held_key = (queries, key_rows)
    grad_probs = jnp.einsum(
        "gihd,gjhd->ghij", grad_heads, value_rows, preferred_element_type=jnp.float32
    )
    grad_scores = probs * (grad_probs - jnp.sum(probs * grad_probs, axis=-1, keepdims=True))
    grad_scores = grad_scores.astype(jnp.bfloat16)
    grad_query = (
        jnp.einsum("ghij,gjhd->gihd", grad_scores, held_key, preferred_element_type=jnp.float32)
        * head_scale
    )
    grad_key = (
        jnp.einsum("ghij,gihd->gjhd", grad_scores, held_query, preferred_element_type=jnp.float32)
        * head_scale
    )
    grad_value = jnp.einsum(
        "ghij,gihd->gjhd", probs_low, grad_heads, preferred_element_type=jnp.float32
    )
    grad_qkv = jnp.stack([grad_query, grad_key, grad_value], axis=2).astype(jnp.bfloat16)
    grad_qkv = grad_qkv.reshape(cell_count, 3 * feature_count)
    grad_grouped = lax.dot_general(
        grad_qkv, qkv_weight, (((1,), (1,)), ((), ())), preferred_element_type=jnp.float32
    ).astype(jnp.bfloat16)
    grad_flat = to_grid(inward(grad_grouped))
    block_out = (state_f + homeward(mixed_flat).astype(jnp.float32)).astype(jnp.bfloat16)
    normalized_gradient = homeward(grad_flat).astype(jnp.float32)
    gain_on_device = jnp.sum(normalized_gradient * standardized_input, axis=(0, 1))
    gain_scaled = normalized_gradient * layer_norm_gain
    layer_norm_gradient = inverse_deviation * (
        gain_scaled
        - jnp.mean(gain_scaled, axis=-1, keepdims=True)
        - standardized_input * jnp.mean(gain_scaled * standardized_input, axis=-1, keepdims=True)
    )
    grad_h = (cotangent.astype(jnp.float32) + layer_norm_gradient).astype(jnp.bfloat16)
    grad_hf = grad_h.astype(jnp.float32)
    padded_grad = widened(grad_h)
    grad_fields = (
        grad_hf + apply_taps(padded_grad, conv_kernel[::-1, ::-1], lat_rows, lon_cols)
    ).astype(jnp.bfloat16)
    kernel_terms = []
    for lat_tap in range(3):
        for lon_tap in range(3):
            kernel_terms.append(
                jnp.sum(
                    padded_fields[lat_tap : lat_tap + lat_rows, lon_tap : lon_tap + lon_cols]
                    * grad_hf,
                    axis=(0, 1),
                )
            )
    kernel_local = jnp.stack(kernel_terms).reshape(3, 3, feature_count)
    gain_total, kernel_total = lax.psum((gain_on_device, kernel_local), ("lat", "lon"))
    return (
        block_out,
        grad_fields,
        grad_project,
        kernel_total * scale_everywhere,
        gain_total * scale_everywhere,
    )


def solution(mesh):
    placed = (
        P("lat", "lon", None),
        P(),
        P(),
        P(),
        P(),
        P(),
        P("lat", "lon", None),
        P("lat", "lon", None),
    )
    return jax.shard_map(
        body,
        mesh=mesh,
        in_specs=placed,
        out_specs=(P("lat", "lon", None), P("lat", "lon", None), P("lat", "lon"), P(), P()),
        check_vma=False,
    )
```

profile of v0, /device:TPU:1, one launch (start us, length us, event | category | flops | bytes accessed | tf_op | source)
XLA Modules:
  0.0 629.2 jit_solution(4152701214273472165)
XLA Ops:
  8.3 2.8 collective-permute-start
  17.3 8.8 %collective-permute-start.2 = (bf16[1,34,768]{2,1,0:T(8,128)(2,1)}, bf16[1,34,768]{2,1,0:T(8,128)(2,1)}, u32[]{:S(2)}, u32[]{:S(2)}) collective-permute-start(bf16[1,34,768]{2,1,0:T(8,128)(2,1)} %get-tuple-element.66), channel_id=1, source_target_pairs={{0,32},{32,64},{64,96},{96,128},{128,160},{160,192},{192,224},{1,3... | collective-permute-start | bytes 156680 | tf_op jit(solution)/shard_map/ppermute | solution.py:20
  27.4 3.2 gather_fusion.2
  30.7 4.7 collective-permute-done.3
  40.1 3.3 gather_fusion
  43.4 2.0 broadcast_select_fusion.1
  45.4 15.7 %all_to_all.108 = bf16[8,32,1,1,1,768]{5,1,4,3,2,0:T(8,128)(2,1)} all-to-all(bf16[8,32,1,1,1,768]{5,1,4,3,2,0:T(8,128)(2,1)S(1)} %bitcast.110), channel_id=1, replica_groups=mesh['lat'=8,'lon'=32] {'lat'}, dimensions={0} | all-to-all | bytes 786432 | tf_op jit(solution)/shard_map/all_to_all | solution.py:45
  61.1 4.1 all-to-all-start
  65.2 2.0 copy.78
  67.2 8.8 %all-to-all-done = bf16[8,32,1,1,1,768]{5,1,4,3,2,0:T(8,128)(2,1)} async-done(((bf16[8,32,1,1,1,768]{5,1,4,3,2,0:T(8,128)(2,1)}), bf16[8,32,1,1,1,768]{5,1,4,3,2,0:T(8,128)(2,1)}, u32[]{:S(2)}, u32[]{:S(2)}) %all-to-all-start) | async-done | bytes 393248 | tf_op jit(solution)/shard_map/all_to_all | solution.py:45
  75.9 17.9 %all-to-all-start.5 = ((bf16[1,32,1,8,1,768]{5,3,4,2,0,1:T(8,128)(2,1)}), bf16[1,32,1,8,1,768]{5,3,4,2,0,1:T(8,128)(2,1)}, u32[]{:S(2)}, u32[]{:S(2)}) async-start(bf16[1,32,1,8,1,768]{5,3,4,2,0,1:T(8,128)(2,1)} %copy.78), calls=%async_computation.5 | async-start | bytes 786432 | tf_op jit(solution)/shard_map/all_to_all | solution.py:44
  95.8 11.9 %all-to-all-done.5 = bf16[1,32,1,8,1,768]{5,3,4,2,0,1:T(8,128)(2,1)} async-done(((bf16[1,32,1,8,1,768]{5,3,4,2,0,1:T(8,128)(2,1)}), bf16[1,32,1,8,1,768]{5,3,4,2,0,1:T(8,128)(2,1)}, u32[]{:S(2)}, u32[]{:S(2)}) %all-to-all-start.5) | async-done | bytes 393248 | tf_op jit(solution)/shard_map/all_to_all | solution.py:44
  107.6 4.8 all-to-all-start.1
  112.5 2.3 copy.71
  116.6 2.5 convolution_convert_fusion.5
  121.0 2.6 reshape.158
  123.6 2.6 all-to-all-done.1
  127.3 2.1 convolution_convert_fusion
  129.4 2.4 copy.67
  131.8 4.6 reshape.150
  136.3 2.6 fusion.58
  145.4 3.2 multiply_reduce_fusion
  150.2 2.5 reshape.151
  152.7 2.7 convolution_convert_fusion.6
  155.4 4.3 all-to-all-start.2
  159.6 3.9 multiply_convert_fusion
  166.4 4.5 copy.86
  170.8 4.5 convert_element_type.159
  175.3 3.1 convolution_convert_fusion.4
  178.5 9.0 %all-to-all-start.6 = ((bf16[1,1,1,8,32,768]{5,4,2,1,0,3:T(8,128)(2,1)}), bf16[1,1,1,8,32,768]{5,4,2,1,0,3:T(8,128)(2,1)}, u32[]{:S(2)}, u32[]{:S(2)}) async-start(bf16[1,1,1,8,32,768]{5,4,2,1,0,3:T(8,128)(2,1)} %bitcast.112), calls=%async_computation.6 | async-start | bytes 786432 | tf_op jit(solution)/shard_map/all_to_all | solution.py:56
  189.5 10.5 %all-to-all-done.6 = bf16[1,1,1,8,32,768]{5,4,2,1,0,3:T(8,128)(2,1)} async-done(((bf16[1,1,1,8,32,768]{5,4,2,1,0,3:T(8,128)(2,1)}), bf16[1,1,1,8,32,768]{5,4,2,1,0,3:T(8,128)(2,1)}, u32[]{:S(2)}, u32[]{:S(2)}) %all-to-all-start.6) | async-done | bytes 393248 | tf_op jit(solution)/shard_map/all_to_all | solution.py:56
  199.9 9.4 %all-to-all-start.3 = ((bf16[8,1,1,1,32,768]{5,0,3,2,1,4:T(8,128)(2,1)}), bf16[8,1,1,1,32,768]{5,0,3,2,1,4:T(8,128)(2,1)}, u32[]{:S(2)}, u32[]{:S(2)}) async-start(bf16[8,1,1,1,32,768]{5,0,3,2,1,4:T(8,128)(2,1)} %copy.75), calls=%async_computation.3 | async-start | bytes 786432 | tf_op jit(solution)/shard_map/all_to_all | solution.py:55
  213.0 2.1 scatter_custom_fusion
  215.1 2.0 copy.88
  217.1 6.0 all-to-all-done.3
  223.1 4.4 all-to-all-start.7
  227.5 2.6 convolution_convert_fusion.1
  234.8 3.4 gather_fusion.1
  238.2 3.0 all-to-all-done.7
  243.0 3.3 gather_fusion.3
  252.8 3.2 fusion.45
  261.2 2.7 stack.59
  267.4 77.1 %all-reduce.1 = (f32[3,3,768]{2,1,0:T(4,128)}, f32[768]{0:T(1024)}) all-reduce(f32[3,3,768]{2,1,0:T(4,128)} %reshape.161, f32[768]{0:T(1024)} %get-tuple-element.35), channel_id=1, replica_groups=mesh['lat'=8,'lon'=32] {'lat','lon'}, use_global_device_ids=true, to_apply=%region_19.21 | all-reduce | flops 7680 | bytes 61440 | tf_op jit(solution)/shard_map/psum | solution.py:194
  346.8 3.8 collective-permute-start.6
  353.1 6.3 collective-permute-done.7
  359.4 2.6 maximum_maximum_fusion.1
  362.1 4.3 fusion.36
  366.4 252.8 %all-reduce.4.cloned.1.call-done = bf16[96,768]{1,0:T(8,128)(2,1)} async-done(((bf16[96,768]{1,0:T(8,128)(2,1)}), bf16[96,768]{1,0:T(8,128)(2,1)}) %all-reduce.4.cloned.1.call-update) | async-done | bytes 147472
  (156 shorter events, 65.3 us)
Async XLA Ops:
  7.2 120.1 %copy-start = (bf16[768,2304]{1,0:T(8,128)(2,1)S(1)}, bf16[768,2304]{1,0:T(8,128)(2,1)}, u32[]{:S(2)}) copy-start(bf16[768,2304]{1,0:T(8,128)(2,1)} %param.13) | copy-start | bytes 10616836
  8.3 6.9 %collective-permute-start = (bf16[8,1,768]{2,1,0:T(2,128)(2,1)S(1)}, bf16[8,1,768]{2,1,0:T(2,128)(2,1)S(1)}, u32[]{:S(2)}, u32[]{:S(2)}) collective-permute-start(bf16[8,1,768]{2,1,0:T(2,128)(2,1)S(1)} %get-tuple-element.71), channel_id=1, source_target_pairs={{0,1},{1,2},{2,3},{3,4},{4,5},{5,6},{6,7},{7,8},{8,9},{9,10},{10,1... | collective-permute-start | bytes 36872 | tf_op jit(solution)/shard_map/ppermute | solution.py:20
  11.1 4.1 collective-permute-start.1
  15.2 23.2 %copy-start.28 = (f32[768]{0:T(1024)}, f32[768]{0:T(1024)S(1)}, u32[]{:S(2)}) copy-start(f32[768]{0:T(1024)S(1)} %get-tuple-element.44) | copy-start | bytes 9220
  15.2 23.2 %copy-start.30 = (f32[768]{0:T(1024)}, f32[768]{0:T(1024)S(1)}, u32[]{:S(2)}) copy-start(f32[768]{0:T(1024)S(1)} %get-tuple-element.45) | copy-start | bytes 9220
  15.8 1.5 copy-start.23
  17.3 13.4 %collective-permute-start.2 = (bf16[1,34,768]{2,1,0:T(8,128)(2,1)}, bf16[1,34,768]{2,1,0:T(8,128)(2,1)}, u32[]{:S(2)}, u32[]{:S(2)}) collective-permute-start(bf16[1,34,768]{2,1,0:T(8,128)(2,1)} %get-tuple-element.66), channel_id=1, source_target_pairs={{0,32},{32,64},{64,96},{96,128},{128,160},{160,192},{192,224},{1,3... | collective-permute-start | bytes 156680 | tf_op jit(solution)/shard_map/ppermute | solution.py:20
  26.1 9.3 %collective-permute-start.3 = (bf16[1,34,768]{2,1,0:T(8,128)(2,1)}, bf16[1,34,768]{2,1,0:T(8,128)(2,1)}, u32[]{:S(2)}, u32[]{:S(2)}) collective-permute-start(bf16[1,34,768]{2,1,0:T(8,128)(2,1)} %get-tuple-element.67), channel_id=1, source_target_pairs={{32,0},{64,32},{96,64},{128,96},{160,128},{192,160},{224,192},{33,... | collective-permute-start | bytes 156680 | tf_op jit(solution)/shard_map/ppermute | solution.py:21
  27.4 3.2 copy-start.40
  30.6 6.5 %copy-start.14 = (bf16[8,32,768]{2,1,0:T(8,128)(2,1)S(1)}, bf16[8,32,768]{2,1,0:T(8,128)(2,1)}, u32[]{:S(2)}) copy-start(bf16[8,32,768]{2,1,0:T(8,128)(2,1)} %param.10) | copy-start | bytes 1179652
  30.6 6.5 %copy-start.21 = (bf16[8,1,768]{2,1,0:T(2,128)(2,1)S(1)}, bf16[8,1,768]{2,1,0:T(2,128)(2,1)}, u32[]{:S(2)}) copy-start(bf16[8,1,768]{2,1,0:T(2,128)(2,1)} %copy-done.20) | copy-start | bytes 36868
  30.6 6.5 %copy-start.24 = (bf16[8,1,768]{2,1,0:T(2,128)(2,1)S(1)}, bf16[8,1,768]{2,1,0:T(2,128)(2,1)}, u32[]{:S(2)}) copy-start(bf16[8,1,768]{2,1,0:T(2,128)(2,1)} %copy-done.23) | copy-start | bytes 36868
  30.6 6.5 %copy-start.32 = (f32[768]{0:T(1024)S(1)}, f32[768]{0:T(1024)}, u32[]{:S(2)}) copy-start(f32[768]{0:T(1024)} %get-tuple-element.46) | copy-start | bytes 9220
  30.6 6.5 %copy-start.34 = (f32[768]{0:T(1024)S(1)}, f32[768]{0:T(1024)}, u32[]{:S(2)}) copy-start(f32[768]{0:T(1024)} %get-tuple-element.47) | copy-start | bytes 9220
  30.6 6.5 %copy-start.35 = (f32[768]{0:T(1024)S(1)}, f32[768]{0:T(1024)}, u32[]{:S(2)}) copy-start(f32[768]{0:T(1024)} %get-tuple-element.48) | copy-start | bytes 9220
  30.6 6.5 %copy-start.36 = (f32[768]{0:T(1024)S(1)}, f32[768]{0:T(1024)}, u32[]{:S(2)}) copy-start(f32[768]{0:T(1024)} %get-tuple-element.49) | copy-start | bytes 9220
  30.6 6.5 %copy-start.37 = (f32[768]{0:T(1024)S(1)}, f32[768]{0:T(1024)}, u32[]{:S(2)}) copy-start(f32[768]{0:T(1024)} %get-tuple-element.50) | copy-start | bytes 9220
  30.7 6.5 %copy-start.38 = (f32[768]{0:T(1024)S(1)}, f32[768]{0:T(1024)}, u32[]{:S(2)}) copy-start(f32[768]{0:T(1024)} %get-tuple-element.51) | copy-start | bytes 9220
  37.2 1.9 copy-start.27
  61.1 14.9 %all-to-all-start = ((bf16[8,32,1,1,1,768]{5,1,4,3,2,0:T(8,128)(2,1)}), bf16[8,32,1,1,1,768]{5,1,4,3,2,0:T(8,128)(2,1)}, u32[]{:S(2)}, u32[]{:S(2)}) async-start(bf16[8,32,1,1,1,768]{5,1,4,3,2,0:T(8,128)(2,1)} %bitcast.109), calls=%async_computation | async-start | bytes 786432 | tf_op jit(solution)/shard_map/all_to_all | solution.py:45
  75.9 31.7 %all-to-all-start.5 = ((bf16[1,32,1,8,1,768]{5,3,4,2,0,1:T(8,128)(2,1)}), bf16[1,32,1,8,1,768]{5,3,4,2,0,1:T(8,128)(2,1)}, u32[]{:S(2)}, u32[]{:S(2)}) async-start(bf16[1,32,1,8,1,768]{5,3,4,2,0,1:T(8,128)(2,1)} %copy.78), calls=%async_computation.5 | async-start | bytes 786432 | tf_op jit(solution)/shard_map/all_to_all | solution.py:44
  107.6 18.6 %all-to-all-start.1 = ((bf16[1,32,1,8,1,768]{5,3,4,2,0,1:T(8,128)(2,1)}), bf16[1,32,1,8,1,768]{5,3,4,2,0,1:T(8,128)(2,1)}, u32[]{:S(2)}, u32[]{:S(2)}) async-start(bf16[1,32,1,8,1,768]{5,3,4,2,0,1:T(8,128)(2,1)} %copy.65), calls=%async_computation.1 | async-start | bytes 786432 | tf_op jit(solution)/shard_map/all_to_all | solution.py:44
  141.2 1.7 copy-start.19
  142.9 2.5 copy-start.6
  142.9 2.5 copy-start.26
  155.4 23.1 %all-to-all-start.2 = ((bf16[1,1,1,8,32,768]{5,4,2,1,0,3:T(8,128)(2,1)}), bf16[1,1,1,8,32,768]{5,4,2,1,0,3:T(8,128)(2,1)}, u32[]{:S(2)}, u32[]{:S(2)}) async-start(bf16[1,1,1,8,32,768]{5,4,2,1,0,3:T(8,128)(2,1)} %bitcast.111), calls=%async_computation.2 | async-start | bytes 786432 | tf_op jit(solution)/shard_map/all_to_all | solution.py:56
  159.6 3.9 copy-start.13
  178.5 21.4 %all-to-all-start.6 = ((bf16[1,1,1,8,32,768]{5,4,2,1,0,3:T(8,128)(2,1)}), bf16[1,1,1,8,32,768]{5,4,2,1,0,3:T(8,128)(2,1)}, u32[]{:S(2)}, u32[]{:S(2)}) async-start(bf16[1,1,1,8,32,768]{5,4,2,1,0,3:T(8,128)(2,1)} %bitcast.112), calls=%async_computation.6 | async-start | bytes 786432 | tf_op jit(solution)/shard_map/all_to_all | solution.py:56
  199.9 23.2 %all-to-all-start.3 = ((bf16[8,1,1,1,32,768]{5,0,3,2,1,4:T(8,128)(2,1)}), bf16[8,1,1,1,32,768]{5,0,3,2,1,4:T(8,128)(2,1)}, u32[]{:S(2)}, u32[]{:S(2)}) async-start(bf16[8,1,1,1,32,768]{5,0,3,2,1,4:T(8,128)(2,1)} %copy.75), calls=%async_computation.3 | async-start | bytes 786432 | tf_op jit(solution)/shard_map/all_to_all | solution.py:55
  223.1 18.1 %all-to-all-start.7 = ((bf16[8,1,1,1,32,768]{5,0,3,2,1,4:T(8,128)(2,1)}), bf16[8,1,1,1,32,768]{5,0,3,2,1,4:T(8,128)(2,1)}, u32[]{:S(2)}, u32[]{:S(2)}) async-start(bf16[8,1,1,1,32,768]{5,0,3,2,1,4:T(8,128)(2,1)} %copy.88), calls=%async_computation.7 | async-start | bytes 786432 | tf_op jit(solution)/shard_map/all_to_all | solution.py:55
  227.5 134.6 %reduce-scatter.3.cloned.1.call-start = ((), (), s32[]{:S(2)}) async-start(), calls=%async_computation.9 | async-start | bytes 1327104 | tf_op jit(solution)/shard_map/reduce_scatter | solution.py:129
  230.2 389.0 %all-reduce.4.cloned.1.call-start = ((), (), s32[]{:S(2)}) async-start(), calls=%async_computation.10 | async-start | bytes 294912
  249.5 1.4 copy-start.9
  249.5 1.4 copy-start.41
  250.8 1.9 copy-start.1
  250.9 1.9 copy-start.3
  250.9 1.9 copy-start.5
  250.9 1.8 copy-start.15
  250.9 1.8 copy-start.22
  250.9 1.8 copy-start.25
  250.9 1.8 copy-start.39
  255.9 106.2 %copy-start.29 = (f32[768]{0:T(1024)S(1)}, f32[768]{0:T(1024)}, u32[]{:S(2)}) copy-start(f32[768]{0:T(1024)} %copy-done.28) | copy-start | bytes 9220
  255.9 106.2 %copy-start.31 = (f32[768]{0:T(1024)S(1)}, f32[768]{0:T(1024)}, u32[]{:S(2)}) copy-start(f32[768]{0:T(1024)} %copy-done.30) | copy-start | bytes 9220
  255.9 106.2 %copy-start.33 = (f32[768]{0:T(1024)S(1)}, f32[768]{0:T(1024)}, u32[]{:S(2)}) copy-start(f32[768]{0:T(1024)} %get-tuple-element.46) | copy-start | bytes 9220
  266.9 79.0 %collective-permute-start.4 = (bf16[8,1,768]{2,1,0:T(2,128)(2,1)}, bf16[8,1,768]{2,1,0:T(2,128)(2,1)}, u32[]{:S(2)}, u32[]{:S(2)}) collective-permute-start(bf16[8,1,768]{2,1,0:T(2,128)(2,1)} %get-tuple-element.68), channel_id=1, source_target_pairs={{0,1},{1,2},{2,3},{3,4},{4,5},{5,6},{6,7},{7,8},{8,9},{9,10},{10,1... | collective-permute-start | bytes 36872 | tf_op jit(solution)/shard_map/ppermute | solution.py:20
  266.9 79.0 %collective-permute-start.5 = (bf16[8,1,768]{2,1,0:T(2,128)(2,1)}, bf16[8,1,768]{2,1,0:T(2,128)(2,1)}, u32[]{:S(2)}, u32[]{:S(2)}) collective-permute-start(bf16[8,1,768]{2,1,0:T(2,128)(2,1)} %get-tuple-element.69), channel_id=1, source_target_pairs={{1,0},{2,1},{3,2},{4,3},{5,4},{6,5},{7,6},{8,7},{9,8},{10,9},{11,1... | collective-permute-start | bytes 36872 | tf_op jit(solution)/shard_map/ppermute | solution.py:21
  346.8 6.4 %collective-permute-start.6 = (bf16[1,34,768]{2,1,0:T(8,128)(2,1)S(1)}, bf16[1,34,768]{2,1,0:T(8,128)(2,1)S(1)}, u32[]{:S(2)}, u32[]{:S(2)}) collective-permute-start(bf16[1,34,768]{2,1,0:T(8,128)(2,1)S(1)} %get-tuple-element.62), channel_id=1, source_target_pairs={{0,32},{32,64},{64,96},{96,128},{128,160},{160,192},{192,224},{1,3... | collective-permute-start | bytes 156680 | tf_op jit(solution)/shard_map/ppermute | solution.py:20
  350.5 8.9 %collective-permute-start.7 = (bf16[1,34,768]{2,1,0:T(8,128)(2,1)S(1)}, bf16[1,34,768]{2,1,0:T(8,128)(2,1)S(1)}, u32[]{:S(2)}, u32[]{:S(2)}) collective-permute-start(bf16[1,34,768]{2,1,0:T(8,128)(2,1)S(1)} %get-tuple-element.63), channel_id=1, source_target_pairs={{32,0},{64,32},{96,64},{128,96},{160,128},{192,160},{224,192},{33,... | collective-permute-start | bytes 156680 | tf_op jit(solution)/shard_map/ppermute | solution.py:21
  (11 other events, 11.6 us)
Sparse Core Ops, SparseCore 0:
  232.3 83.6 reduce-scatter.2
  362.2 256.9 all-reduce.3
where the time goes:
time: 638 us; the launch traced here: 629 us
  waiting for transfers between devices  307 us (48%)
  blocking collectives  92.7 us (15%)
  local copies, waits for them, and re-layouts  80.9 us (13%)
  starting transfers between devices  73.1 us (11%)
  other arithmetic  39.4 us (6%)
  matrix products  20.8 us (3%)
  between operations  15.6 us (2%)
    unnamed x3, waiting for transfers between devices  253 us
    psum x1, blocking collectives, body(): lax.psum((gain_on_device, kernel_local), ('lat', 'lon'))  77.1 us
    all_to_all x2, starting transfers between devices, to_owner(): lax.all_to_all(lax.all_to_all(packed, 'lat', split_axis=0, concat_axis=3,...  22.7 us
    all_to_all x1, blocking collectives, to_owner(): lax.all_to_all(packed, 'lat', split_axis=0, concat_axis=3, tiled=True)  15.7 us
    ppermute x4, starting transfers between devices, extended(): before = lax.ppermute(last, axis, up)  15.3 us
    all_to_all x2, waiting for transfers between devices, to_owner(): lax.all_to_all(lax.all_to_all(packed, 'lat', split_axis=0, concat_axis=3,...  14.5 us
    all_to_all x2, starting transfers between devices, to_grid(): lax.all_to_all(lax.all_to_all(packed, 'lat', split_axis=3, concat_axis=0,...  13.7 us
    all_to_all x2, starting transfers between devices, to_grid(): lax.all_to_all(packed, 'lat', split_axis=3, concat_axis=0, tiled=True)  13.3 us
  transfers between devices with their start and end apart: 17, of which 9 were waited for; matrix products, arithmetic and copies ran while one was open for 15% of the time, Pallas kernels for 0%

commit v1 on v0

--- a/solution.py
+++ b/solution.py
@@ -191,7 +191,7 @@
                 )
             )
     kernel_local = jnp.stack(kernel_terms).reshape(3, 3, feature_count)
-    gain_total, kernel_total = lax.psum((gain_on_device, kernel_local), ("lat", "lon"))
+    gain_total, kernel_total = lax.psum(lax.psum((gain_on_device, kernel_local), "lon"), "lat")
     return (
         block_out,
         grad_fields,

time: 638 us -> 744 us (1.17)
  blocking collectives: 92.7 us -> 191 us
    psum x1 -> x2, blocking collectives: 77.1 us -> 175 us  [the longest x1 133 us: body(): lax.psum((gain_on_device, kernel_local), 'lon')]
  transfers between devices with their start and end apart: 17 -> 17, of which waited for: 9 -> 9; matrix products, arithmetic and copies ran while one was open for 15% -> 13% of each run, Pallas kernels for 0% -> 0%
where the time goes in v1:
time: 744 us; the launch traced here: 735 us
  waiting for transfers between devices  314 us (42%)
  blocking collectives  191 us (26%)
  local copies, waits for them, and re-layouts  80.9 us (11%)
  starting transfers between devices  74.5 us (10%)
  other arithmetic  39.4 us (5%)
  matrix products  20.8 us (3%)
  between operations  15.6 us (2%)
    unnamed x3, waiting for transfers between devices  260 us
    psum x1, blocking collectives, body(): lax.psum((gain_on_device, kernel_local), 'lon')  133 us
    psum x1, blocking collectives, body(): lax.psum(lax.psum((gain_on_device, kernel_local), 'lon'), 'lat')  42.2 us
    all_to_all x2, starting transfers between devices, to_owner(): lax.all_to_all(lax.all_to_all(packed, 'lat', split_axis=0, concat_axis=3,...  22.7 us
    ppermute x4, starting transfers between devices, extended(): before = lax.ppermute(last, axis, up)  16.7 us
    all_to_all x1, blocking collectives, to_owner(): lax.all_to_all(packed, 'lat', split_axis=0, concat_axis=3, tiled=True)  15.7 us
  transfers between devices with their start and end apart: 17, of which 9 were waited for; matrix products, arithmetic and copies ran while one was open for 13% of the time, Pallas kernels for 0%

profile of v1, /device:TPU:1, one launch (start us, length us, event | category | flops | bytes accessed | tf_op | source)
XLA Modules:
  0.0 735.4 jit_solution(12968204848414138158)
XLA Ops:
  8.3 2.8 collective-permute-start
  17.3 8.8 %collective-permute-start.2 = (bf16[1,34,768]{2,1,0:T(8,128)(2,1)}, bf16[1,34,768]{2,1,0:T(8,128)(2,1)}, u32[]{:S(2)}, u32[]{:S(2)}) collective-permute-start(bf16[1,34,768]{2,1,0:T(8,128)(2,1)} %get-tuple-element.68), channel_id=1, source_target_pairs={{0,32},{32,64},{64,96},{96,128},{128,160},{160,192},{192,224},{1,3... | collective-permute-start | bytes 156680 | tf_op jit(solution)/shard_map/ppermute | solution.py:20
  27.4 3.2 gather_fusion.2
  30.7 4.7 collective-permute-done.3
  40.1 3.3 gather_fusion
  43.4 2.0 broadcast_select_fusion.1
  45.4 15.7 %all_to_all.108 = bf16[8,32,1,1,1,768]{5,1,4,3,2,0:T(8,128)(2,1)} all-to-all(bf16[8,32,1,1,1,768]{5,1,4,3,2,0:T(8,128)(2,1)S(1)} %bitcast.110), channel_id=1, replica_groups=mesh['lat'=8,'lon'=32] {'lat'}, dimensions={0} | all-to-all | bytes 786432 | tf_op jit(solution)/shard_map/all_to_all | solution.py:45
  61.1 4.1 all-to-all-start
  65.2 2.0 copy.78
  67.2 8.8 %all-to-all-done = bf16[8,32,1,1,1,768]{5,1,4,3,2,0:T(8,128)(2,1)} async-done(((bf16[8,32,1,1,1,768]{5,1,4,3,2,0:T(8,128)(2,1)}), bf16[8,32,1,1,1,768]{5,1,4,3,2,0:T(8,128)(2,1)}, u32[]{:S(2)}, u32[]{:S(2)}) %all-to-all-start) | async-done | bytes 393248 | tf_op jit(solution)/shard_map/all_to_all | solution.py:45
  75.9 17.9 %all-to-all-start.5 = ((bf16[1,32,1,8,1,768]{5,3,4,2,0,1:T(8,128)(2,1)}), bf16[1,32,1,8,1,768]{5,3,4,2,0,1:T(8,128)(2,1)}, u32[]{:S(2)}, u32[]{:S(2)}) async-start(bf16[1,32,1,8,1,768]{5,3,4,2,0,1:T(8,128)(2,1)} %copy.78), calls=%async_computation.5 | async-start | bytes 786432 | tf_op jit(solution)/shard_map/all_to_all | solution.py:44
  95.8 11.9 %all-to-all-done.5 = bf16[1,32,1,8,1,768]{5,3,4,2,0,1:T(8,128)(2,1)} async-done(((bf16[1,32,1,8,1,768]{5,3,4,2,0,1:T(8,128)(2,1)}), bf16[1,32,1,8,1,768]{5,3,4,2,0,1:T(8,128)(2,1)}, u32[]{:S(2)}, u32[]{:S(2)}) %all-to-all-start.5) | async-done | bytes 393248 | tf_op jit(solution)/shard_map/all_to_all | solution.py:44
  107.6 4.8 all-to-all-start.1
  112.5 2.3 copy.71
  116.6 2.5 convolution_convert_fusion.5
  121.0 2.6 reshape.158
  123.6 2.6 all-to-all-done.1
  127.3 2.1 convolution_convert_fusion
  129.4 2.4 copy.67
  131.8 4.6 reshape.150
  136.3 2.6 fusion.58
  145.4 3.2 multiply_reduce_fusion
  150.2 2.5 reshape.151
  152.7 2.7 convolution_convert_fusion.6
  155.4 4.3 all-to-all-start.2
  159.6 3.9 multiply_convert_fusion
  166.4 4.5 copy.86
  170.8 4.5 convert_element_type.159
  175.3 3.1 convolution_convert_fusion.4
  178.5 9.0 %all-to-all-start.6 = ((bf16[1,1,1,8,32,768]{5,4,2,1,0,3:T(8,128)(2,1)}), bf16[1,1,1,8,32,768]{5,4,2,1,0,3:T(8,128)(2,1)}, u32[]{:S(2)}, u32[]{:S(2)}) async-start(bf16[1,1,1,8,32,768]{5,4,2,1,0,3:T(8,128)(2,1)} %bitcast.112), calls=%async_computation.6 | async-start | bytes 786432 | tf_op jit(solution)/shard_map/all_to_all | solution.py:56
  189.5 10.5 %all-to-all-done.6 = bf16[1,1,1,8,32,768]{5,4,2,1,0,3:T(8,128)(2,1)} async-done(((bf16[1,1,1,8,32,768]{5,4,2,1,0,3:T(8,128)(2,1)}), bf16[1,1,1,8,32,768]{5,4,2,1,0,3:T(8,128)(2,1)}, u32[]{:S(2)}, u32[]{:S(2)}) %all-to-all-start.6) | async-done | bytes 393248 | tf_op jit(solution)/shard_map/all_to_all | solution.py:56
  199.9 9.4 %all-to-all-start.3 = ((bf16[8,1,1,1,32,768]{5,0,3,2,1,4:T(8,128)(2,1)}), bf16[8,1,1,1,32,768]{5,0,3,2,1,4:T(8,128)(2,1)}, u32[]{:S(2)}, u32[]{:S(2)}) async-start(bf16[8,1,1,1,32,768]{5,0,3,2,1,4:T(8,128)(2,1)} %copy.75), calls=%async_computation.3 | async-start | bytes 786432 | tf_op jit(solution)/shard_map/all_to_all | solution.py:55
  213.0 2.1 scatter_custom_fusion
  217.1 6.0 all-to-all-done.3
  223.1 4.4 all-to-all-start.7
  227.5 2.6 convolution_convert_fusion.1
  234.8 3.4 gather_fusion.1
  238.2 3.0 all-to-all-done.7
  243.0 3.3 gather_fusion.3
  252.8 3.2 fusion.45
  261.2 2.7 stack.59
  267.4 132.6 %all-reduce.1 = (f32[3,3,768]{2,1,0:T(4,128)}, f32[768]{0:T(1024)}) all-reduce(f32[3,3,768]{2,1,0:T(4,128)} %reshape.161, f32[768]{0:T(1024)} %get-tuple-element.35), channel_id=1, replica_groups=mesh['lat'=8,'lon'=32] {'lon'}, use_global_device_ids=true, to_apply=%region_19.21 | all-reduce | flops 7680 | bytes 61440 | tf_op jit(solution)/shard_map/psum | solution.py:194
  400.1 42.2 %all-reduce.2 = (f32[3,3,768]{2,1,0:T(4,128)}, f32[768]{0:T(1024)}) all-reduce(f32[3,3,768]{2,1,0:T(4,128)} %get-tuple-element.52, f32[768]{0:T(1024)} %get-tuple-element.53), channel_id=1, replica_groups=mesh['lat'=8,'lon'=32] {'lat'}, use_global_device_ids=true, to_apply=%region_20.22 | all-reduce | flops 7680 | bytes 61440 | tf_op jit(solution)/shard_map/psum | solution.py:194
  444.6 5.1 collective-permute-start.6
  452.3 6.3 collective-permute-done.7
  458.6 2.6 maximum_maximum_fusion.1
  461.3 4.3 fusion.36
  465.6 259.8 %all-reduce.5.cloned.1.call-done = bf16[96,768]{1,0:T(8,128)(2,1)} async-done(((bf16[96,768]{1,0:T(8,128)(2,1)}), bf16[96,768]{1,0:T(8,128)(2,1)}) %all-reduce.5.cloned.1.call-update) | async-done | bytes 147472
  (157 shorter events, 67.3 us)
Async XLA Ops:
  7.2 120.1 %copy-start = (bf16[768,2304]{1,0:T(8,128)(2,1)S(1)}, bf16[768,2304]{1,0:T(8,128)(2,1)}, u32[]{:S(2)}) copy-start(bf16[768,2304]{1,0:T(8,128)(2,1)} %param.13) | copy-start | bytes 10616836
  8.3 6.9 collective-permute-start
  11.1 4.1 collective-permute-start.1
  15.2 23.2 %copy-start.28 = (f32[768]{0:T(1024)}, f32[768]{0:T(1024)S(1)}, u32[]{:S(2)}) copy-start(f32[768]{0:T(1024)S(1)} %get-tuple-element.44) | copy-start | bytes 9220
  15.2 23.2 %copy-start.30 = (f32[768]{0:T(1024)}, f32[768]{0:T(1024)S(1)}, u32[]{:S(2)}) copy-start(f32[768]{0:T(1024)S(1)} %get-tuple-element.45) | copy-start | bytes 9220
  15.8 1.5 copy-start.23
  17.3 13.4 %collective-permute-start.2 = (bf16[1,34,768]{2,1,0:T(8,128)(2,1)}, bf16[1,34,768]{2,1,0:T(8,128)(2,1)}, u32[]{:S(2)}, u32[]{:S(2)}) collective-permute-start(bf16[1,34,768]{2,1,0:T(8,128)(2,1)} %get-tuple-element.68), channel_id=1, source_target_pairs={{0,32},{32,64},{64,96},{96,128},{128,160},{160,192},{192,224},{1,3... | collective-permute-start | bytes 156680 | tf_op jit(solution)/shard_map/ppermute | solution.py:20
  26.1 9.3 %collective-permute-start.3 = (bf16[1,34,768]{2,1,0:T(8,128)(2,1)}, bf16[1,34,768]{2,1,0:T(8,128)(2,1)}, u32[]{:S(2)}, u32[]{:S(2)}) collective-permute-start(bf16[1,34,768]{2,1,0:T(8,128)(2,1)} %get-tuple-element.69), channel_id=1, source_target_pairs={{32,0},{64,32},{96,64},{128,96},{160,128},{192,160},{224,192},{33,... | collective-permute-start | bytes 156680 | tf_op jit(solution)/shard_map/ppermute | solution.py:21
  27.4 3.2 copy-start.40
  30.6 6.5 copy-start.14
  30.6 6.5 copy-start.21
  30.6 6.5 copy-start.24
  30.6 6.5 copy-start.32
  30.6 6.5 copy-start.34
  30.6 6.5 copy-start.35
  30.6 6.5 copy-start.36
  30.6 6.5 copy-start.37
  30.7 6.5 copy-start.38
  37.2 1.9 copy-start.27
  61.1 14.9 %all-to-all-start = ((bf16[8,32,1,1,1,768]{5,1,4,3,2,0:T(8,128)(2,1)}), bf16[8,32,1,1,1,768]{5,1,4,3,2,0:T(8,128)(2,1)}, u32[]{:S(2)}, u32[]{:S(2)}) async-start(bf16[8,32,1,1,1,768]{5,1,4,3,2,0:T(8,128)(2,1)} %bitcast.109), calls=%async_computation | async-start | bytes 786432 | tf_op jit(solution)/shard_map/all_to_all | solution.py:45
  75.9 31.7 %all-to-all-start.5 = ((bf16[1,32,1,8,1,768]{5,3,4,2,0,1:T(8,128)(2,1)}), bf16[1,32,1,8,1,768]{5,3,4,2,0,1:T(8,128)(2,1)}, u32[]{:S(2)}, u32[]{:S(2)}) async-start(bf16[1,32,1,8,1,768]{5,3,4,2,0,1:T(8,128)(2,1)} %copy.78), calls=%async_computation.5 | async-start | bytes 786432 | tf_op jit(solution)/shard_map/all_to_all | solution.py:44
  107.6 18.6 %all-to-all-start.1 = ((bf16[1,32,1,8,1,768]{5,3,4,2,0,1:T(8,128)(2,1)}), bf16[1,32,1,8,1,768]{5,3,4,2,0,1:T(8,128)(2,1)}, u32[]{:S(2)}, u32[]{:S(2)}) async-start(bf16[1,32,1,8,1,768]{5,3,4,2,0,1:T(8,128)(2,1)} %copy.65), calls=%async_computation.1 | async-start | bytes 786432 | tf_op jit(solution)/shard_map/all_to_all | solution.py:44
  141.2 1.7 copy-start.19
  142.9 2.5 copy-start.6
  142.9 2.5 copy-start.26
  155.4 23.1 %all-to-all-start.2 = ((bf16[1,1,1,8,32,768]{5,4,2,1,0,3:T(8,128)(2,1)}), bf16[1,1,1,8,32,768]{5,4,2,1,0,3:T(8,128)(2,1)}, u32[]{:S(2)}, u32[]{:S(2)}) async-start(bf16[1,1,1,8,32,768]{5,4,2,1,0,3:T(8,128)(2,1)} %bitcast.111), calls=%async_computation.2 | async-start | bytes 786432 | tf_op jit(solution)/shard_map/all_to_all | solution.py:56
  159.6 3.9 copy-start.13
  178.5 21.4 %all-to-all-start.6 = ((bf16[1,1,1,8,32,768]{5,4,2,1,0,3:T(8,128)(2,1)}), bf16[1,1,1,8,32,768]{5,4,2,1,0,3:T(8,128)(2,1)}, u32[]{:S(2)}, u32[]{:S(2)}) async-start(bf16[1,1,1,8,32,768]{5,4,2,1,0,3:T(8,128)(2,1)} %bitcast.112), calls=%async_computation.6 | async-start | bytes 786432 | tf_op jit(solution)/shard_map/all_to_all | solution.py:56
  199.9 23.2 %all-to-all-start.3 = ((bf16[8,1,1,1,32,768]{5,0,3,2,1,4:T(8,128)(2,1)}), bf16[8,1,1,1,32,768]{5,0,3,2,1,4:T(8,128)(2,1)}, u32[]{:S(2)}, u32[]{:S(2)}) async-start(bf16[8,1,1,1,32,768]{5,0,3,2,1,4:T(8,128)(2,1)} %copy.75), calls=%async_computation.3 | async-start | bytes 786432 | tf_op jit(solution)/shard_map/all_to_all | solution.py:55
  223.1 18.1 %all-to-all-start.7 = ((bf16[8,1,1,1,32,768]{5,0,3,2,1,4:T(8,128)(2,1)}), bf16[8,1,1,1,32,768]{5,0,3,2,1,4:T(8,128)(2,1)}, u32[]{:S(2)}, u32[]{:S(2)}) async-start(bf16[8,1,1,1,32,768]{5,0,3,2,1,4:T(8,128)(2,1)} %copy.88), calls=%async_computation.7 | async-start | bytes 786432 | tf_op jit(solution)/shard_map/all_to_all | solution.py:55
  227.5 233.7 %reduce-scatter.3.cloned.1.call-start = ((), (), s32[]{:S(2)}) async-start(), calls=%async_computation.9 | async-start | bytes 1327104 | tf_op jit(solution)/shard_map/reduce_scatter | solution.py:129
  230.2 495.2 %all-reduce.5.cloned.1.call-start = ((), (), s32[]{:S(2)}) async-start(), calls=%async_computation.10 | async-start | bytes 294912
  249.5 1.4 copy-start.9
  249.5 1.4 copy-start.41
  250.8 1.9 copy-start.1
  250.9 1.9 copy-start.3
  250.9 1.9 copy-start.5
  250.9 1.8 copy-start.15
  250.9 1.8 copy-start.22
  250.9 1.8 copy-start.25
  250.9 1.8 copy-start.39
  255.9 205.3 %copy-start.29 = (f32[768]{0:T(1024)S(1)}, f32[768]{0:T(1024)}, u32[]{:S(2)}) copy-start(f32[768]{0:T(1024)} %copy-done.28) | copy-start | bytes 9220
  255.9 205.3 %copy-start.31 = (f32[768]{0:T(1024)S(1)}, f32[768]{0:T(1024)}, u32[]{:S(2)}) copy-start(f32[768]{0:T(1024)} %copy-done.30) | copy-start | bytes 9220
  255.9 205.3 %copy-start.33 = (f32[768]{0:T(1024)S(1)}, f32[768]{0:T(1024)}, u32[]{:S(2)}) copy-start(f32[768]{0:T(1024)} %get-tuple-element.46) | copy-start | bytes 9220
  266.9 176.8 %collective-permute-start.4 = (bf16[8,1,768]{2,1,0:T(2,128)(2,1)}, bf16[8,1,768]{2,1,0:T(2,128)(2,1)}, u32[]{:S(2)}, u32[]{:S(2)}) collective-permute-start(bf16[8,1,768]{2,1,0:T(2,128)(2,1)} %get-tuple-element.70), channel_id=1, source_target_pairs={{0,1},{1,2},{2,3},{3,4},{4,5},{5,6},{6,7},{7,8},{8,9},{9,10},{10,1... | collective-permute-start | bytes 36872 | tf_op jit(solution)/shard_map/ppermute | solution.py:20
  266.9 176.8 %collective-permute-start.5 = (bf16[8,1,768]{2,1,0:T(2,128)(2,1)}, bf16[8,1,768]{2,1,0:T(2,128)(2,1)}, u32[]{:S(2)}, u32[]{:S(2)}) collective-permute-start(bf16[8,1,768]{2,1,0:T(2,128)(2,1)} %get-tuple-element.71), channel_id=1, source_target_pairs={{1,0},{2,1},{3,2},{4,3},{5,4},{6,5},{7,6},{8,7},{9,8},{10,9},{11,1... | collective-permute-start | bytes 36872 | tf_op jit(solution)/shard_map/ppermute | solution.py:21
  444.6 7.7 %collective-permute-start.6 = (bf16[1,34,768]{2,1,0:T(8,128)(2,1)S(1)}, bf16[1,34,768]{2,1,0:T(8,128)(2,1)S(1)}, u32[]{:S(2)}, u32[]{:S(2)}) collective-permute-start(bf16[1,34,768]{2,1,0:T(8,128)(2,1)S(1)} %get-tuple-element.64), channel_id=1, source_target_pairs={{0,32},{32,64},{64,96},{96,128},{128,160},{160,192},{192,224},{1,3... | collective-permute-start | bytes 156680 | tf_op jit(solution)/shard_map/ppermute | solution.py:20
  449.7 8.9 %collective-permute-start.7 = (bf16[1,34,768]{2,1,0:T(8,128)(2,1)S(1)}, bf16[1,34,768]{2,1,0:T(8,128)(2,1)S(1)}, u32[]{:S(2)}, u32[]{:S(2)}) collective-permute-start(bf16[1,34,768]{2,1,0:T(8,128)(2,1)S(1)} %get-tuple-element.65), channel_id=1, source_target_pairs={{32,0},{64,32},{96,64},{128,96},{160,128},{192,160},{224,192},{33,... | collective-permute-start | bytes 156680 | tf_op jit(solution)/shard_map/ppermute | solution.py:21
  (11 other events, 11.6 us)
Sparse Core Ops, SparseCore 0:
  232.3 83.5 reduce-scatter.2
  461.4 263.9 all-reduce.4
